TPU v7x, 32 devices: a whole 2x2x4 slice. The times are simulated.
32 devices in a mesh: parts: 2 (over x), chol: 16 (over z, y, core).
Axes of the slice: x: 2, y: 2, z: 4, core: 2. Of those that a mesh axis runs over, the one named last changes fastest.
Arguments:
- orbitals: float32 [32, 100, 1024], P(('parts', 'chol')), parts along dimension 0, may hold values from -6 to 6
- intersection_inv: float32 [32, 100, 100], P(('parts', 'chol')), parts along dimension 0, may hold values from -0.625 to 0.625
- factor_rows: bfloat16 [4096, 1024], P('chol'), may hold values from -0.1875 to 0.1875
- factor_rotated: bfloat16 [100, 4096], replicated, may hold values from -0.625 to 0.625
- factor_core: bfloat16 [1024, 4096], P('chol'), may hold values from -0.125 to 0.125
- fields: float32 [32, 1024], P('parts', 'chol'), parts along dimension 0, may hold values from -6 to 6
Outputs:
- propagated: float32 [32, 100, 1024], P(('parts', 'chol')), parts along dimension 0
- force_bias: float32 [32, 1024], P('parts', 'chol'), parts along dimension 0
There are 2 independent parts, one for each index of `parts`. A program takes and returns all parts, laid end to end along the dimension named above; an argument that names none is the same for every part. Nothing has to cross between parts.
All inputs are finite; a program needn't handle non-finite values.
Results may differ from a plain program's by a relative error of at most 0.0091.
Values may be sent and summed in bfloat16 or wider, within the bound.
A program may use at most 64 MiB of HBM per device.

v0:
```python
import jax
import jax.numpy as jnp
from jax import lax
from jax.sharding import PartitionSpec as P

TAYLOR = 4


def density_one(half_green, all_rows, factor_rotated):
    projected = lax.dot_general(
        half_green, all_rows, (((1,), (1,)), ((), ())), preferred_element_type=jnp.float32
    )
    return jnp.sum(factor_rotated.astype(jnp.float32) * projected, axis=0).astype(jnp.bfloat16)


def propagate_one(orbital, potential, all_rows):
    total = orbital
    term = orbital
    for order in range(1, TAYLOR + 1):
        summed = lax.dot_general(
            term.astype(jnp.bfloat16),
            all_rows,
            (((1,), (1,)), ((), ())),
            preferred_element_type=jnp.float32,
        )
        scaled = (summed * potential[None, :] / order).astype(jnp.bfloat16)
        term = jnp.dot(scaled, all_rows, preferred_element_type=jnp.float32)
        total = total + term
    return total


def on_device(orbitals, intersection_inv, factor_rows, factor_rotated, factor_core, fields):
    walker_count = orbitals.shape[0]
    half_green = jnp.einsum(
        "wij,wjm->wim", intersection_inv, orbitals, precision=lax.Precision.HIGHEST
    ).astype(jnp.bfloat16)
    all_rows = lax.all_gather(factor_rows, "chol", axis=0, tiled=True)
    own_density = lax.map(lambda item: density_one(item, all_rows, factor_rotated), half_green)
    density = lax.all_gather(own_density, "chol", axis=0, tiled=True)
    force_bias = lax.dot_general(
        density, factor_core, (((1,), (1,)), ((), ())), preferred_element_type=jnp.float32
    )
    shifted = (fields - force_bias).astype(jnp.bfloat16)
    partial_sum = jnp.dot(shifted, factor_core, preferred_element_type=jnp.float32)
    summed_all = lax.psum(partial_sum, "chol")
    potential = lax.dynamic_slice_in_dim(
        summed_all, lax.axis_index("chol") * walker_count, walker_count, 0
    )
    propagated = lax.map(
        lambda pair: propagate_one(pair[0], pair[1], all_rows), (orbitals, potential)
    )
    return (propagated, force_bias)


def solution(mesh):
    in_specs = (
        P(("parts", "chol"), None, None),
        P(("parts", "chol"), None, None),
        P("chol", None),
        P(),
        P("chol", None),
        P("parts", "chol"),
    )
    out_specs = (P(("parts", "chol"), None, None), P("parts", "chol"))
    return jax.shard_map(
        on_device, mesh=mesh, in_specs=in_specs, out_specs=out_specs, check_vma=False
    )
```

profile of v0, /device:TPU:0, one launch (start us, length us, event | category | flops | bytes accessed | tf_op | source)
XLA Modules:
  0.0 249.2 jit_solution(8666170632495442712)
XLA Ops:
  7.2 0.0 copy-start
  7.2 0.0 copy-start.1
  7.2 0.0 copy-start.3
  7.2 0.0 all-gather.3.cloned.1.call-start
  7.2 0.7 all-gather.3.cloned.1.call-update
  7.9 0.0 all-reduce.2.cloned.1.call-start
  8.0 1.6 convolution_convert_fusion
  9.6 77.7 %all-gather.3.cloned.1.call-done = bf16[4096,1024]{1,0:T(8,128)(2,1)} async-done(((bf16[256,1024]{1,0:T(8,128)(2,1)}), bf16[4096,1024]{1,0:T(8,128)(2,1)}) %all-gather.3.cloned.1.call-update) | async-done | bytes 8388624 | tf_op jit(solution)/shard_map/all_gather | solution.py:37
  87.2 6.3 %fusion.7 = bf16[4096]{0:T(1024)(128)(2,1)S(1)} fusion(bf16[100,1024]{1,0:T(8,128)(2,1)S(1)} %convolution_convert_fusion, bf16[4096,1024]{1,0:T(8,128)(2,1)} %all-gather.3.cloned.1.call-done, bf16[100,4096]{1,0:T(8,128)(2,1)} %param.9), kind=kOutput, calls=%fused_computation.12 | convolution fusion | flops 840085504 | bytes 9420800 | tf_op jit(solution)/shard_map/while/body/eval_jaxpr/dot_general | solution.py:10
  93.5 19.5 %all-gather = bf16[65536]{0:T(1024)(128)(2,1)S(1)} all-gather(bf16[4096]{0:T(1024)(128)(2,1)S(1)} %fusion.7), channel_id=2, replica_groups=mesh['parts'=2,'chol'=16] {'chol'}, dimensions={0}, use_global_device_ids=true | all-gather | bytes 139264 | tf_op jit(solution)/shard_map/all_gather | solution.py:39
  113.0 0.1 reshape.20
  113.1 0.0 copy-done
  113.1 0.2 fusion.28
  113.3 0.0 copy-done.3
  113.3 0.0 copy-start.2
  113.3 0.9 fusion.24
  114.2 0.0 all-reduce.2.cloned.1.call-update
  114.3 87.1 %all-reduce.2.cloned.1.call-done = f32[16,4096]{1,0:T(8,128)} async-done(((f32[16,4096]{1,0:T(8,128)}), f32[16,4096]{1,0:T(8,128)}) %all-reduce.2.cloned.1.call-update) | async-done | bytes 262160 | tf_op jit(solution)/shard_map/psum | solution.py:45
  201.4 0.9 constant_dynamic-slice_fusion
  202.3 0.0 copy-done.1
  202.3 9.7 %fusion.11 = f32[100,1024]{1,0:T(8,128)S(1)} fusion(bf16[4096,1024]{1,0:T(8,128)(2,1)} %all-gather.3.cloned.1.call-done, f32[4096]{0:T(1024)S(1)} %bitcast.32, f32[1,100,1024]{2,0,1:T(1,128)S(1)} %copy-done.1), kind=kOutput, calls=%fused_computation.18 | convolution fusion | flops 1678540800 | bytes 9224192 | tf_op jit(solution)/shard_map/while/body/eval_jaxpr/dot_general | solution.py:27
  212.0 0.0 copy-done.2
  212.0 9.7 %fusion.10 = f32[100,1024]{1,0:T(8,128)S(1)} fusion(bf16[4096,1024]{1,0:T(8,128)(2,1)} %all-gather.3.cloned.1.call-done, f32[4096]{0:T(1024)S(1)} %bitcast.33, f32[100,1024]{1,0:T(8,128)S(1)} %fusion.11), kind=kOutput, calls=%fused_computation.17 | convolution fusion | flops 1679052800 | bytes 9224192 | tf_op jit(solution)/shard_map/while/body/eval_jaxpr/dot_general | solution.py:27
  221.7 9.7 %fusion.9 = f32[100,1024]{1,0:T(8,128)S(1)} fusion(bf16[4096,1024]{1,0:T(8,128)(2,1)} %all-gather.3.cloned.1.call-done, f32[4096]{0:T(1024)S(1)} %bitcast.34, f32[100,1024]{1,0:T(8,128)S(1)} %fusion.10), kind=kOutput, calls=%fused_computation.16 | convolution fusion | flops 1679052800 | bytes 9224192 | tf_op jit(solution)/shard_map/while/body/eval_jaxpr/dot_general | solution.py:27
  231.5 9.7 %fusion.8 = f32[1,100,1024]{2,1,0:T(8,128)S(1)} fusion(bf16[4096,1024]{1,0:T(8,128)(2,1)} %all-gather.3.cloned.1.call-done, f32[4096]{0:T(1024)S(1)} %bitcast.35, f32[100,1024]{1,0:T(8,128)S(1)} %fusion.9, f32[100,1024]{1,0:T(8,128)S(1)} %fusion.10, f32[100,1024]{1,0:T(8,128)S(1)} %fusion.11, f32[1,100,1024]{2,0,1:T(1,128)S(1)} %copy-done.1), kind=kOutput, calls=%fused_computation.14 | convolution fusion | flops 1679462400 | bytes 10452992 | tf_op jit(solution)/shard_map/while/body/eval_jaxpr/dot_general | solution.py:27
  241.2 1.2 copy.9
Async XLA Ops:
  7.2 105.9 %copy-start = (bf16[64,4096]{1,0:T(8,128)(2,1)S(1)}, bf16[64,4096]{1,0:T(8,128)(2,1)}, u32[]{:S(2)}) copy-start(bf16[64,4096]{1,0:T(8,128)(2,1)} %param.10) | copy-start | bytes 1572868
  7.2 195.2 %copy-start.1 = (f32[1,100,1024]{2,0,1:T(1,128)S(1)}, f32[1,100,1024]{2,0,1:T(1,128)}, u32[]{:S(2)}) copy-start(f32[1,100,1024]{2,0,1:T(1,128)} %param.6) | copy-start | bytes 1228804
  7.2 106.1 %copy-start.3 = (f32[16,64]{1,0:T(8,128)S(1)}, f32[16,64]{1,0:T(8,128)}, u32[]{:S(2)}) copy-start(f32[16,64]{1,0:T(8,128)} %param.11) | copy-start | bytes 12292
  7.2 80.0 %all-gather.3.cloned.1.call-start = ((), (), s32[]{:S(2)}) async-start(), calls=%async_computation | async-start | bytes 8912896 | tf_op jit(solution)/shard_map/all_gather | solution.py:37
  7.9 193.5 %all-reduce.2.cloned.1.call-start = ((), (), s32[]{:S(2)}) async-start(), calls=%async_computation.1 | async-start | bytes 524288 | tf_op jit(solution)/shard_map/psum | solution.py:45
  113.3 98.7 %copy-start.2 = (f32[16,64]{1,0:T(8,128)}, f32[16,64]{1,0:T(8,128)S(1)}, u32[]{:S(2)}) copy-start(f32[16,64]{1,0:T(8,128)S(1)} %fusion.28) | copy-start | bytes 12292
Sparse Core Ops, SparseCore 0:
  10.2 77.0 all-gather.2
  114.4 86.9 all-reduce.1
where the time goes:
time: 249 us
  waiting for transfers between devices  166 us (67%)
  matrix products  47.9 us (19%)
  blocking collectives  19.5 us (8%)
  between operations  14.1 us (6%)
    psum x1, waiting for transfers between devices, on_device(): summed_all = lax.psum(partial_sum, 'chol')  87.1 us
    all_gather x1, waiting for transfers between devices, on_device(): all_rows = lax.all_gather(factor_rows, 'chol', axis=0, tiled=True)  77.7 us
    dot_general x4, matrix products, propagate_one(): term = jnp.dot(scaled, all_rows, preferred_element_type=jnp.float32)  38.9 us
    all_gather x1, blocking collectives, on_device(): density = lax.all_gather(own_density, 'chol', axis=0, tiled=True)  19.5 us
    dot_general x1, matrix products, density_one(): lax.dot_general(half_green, all_rows, (((1,), (1,)), ((), ())), preferred...  6.26 us
  transfers between devices with their start and end apart: 2, of which 2 were waited for; matrix products, arithmetic and copies ran while one was open for 1% of the time, Pallas kernels for 0%

commit v1 on v0

--- a/solution.py
+++ b/solution.py
@@ -34,7 +34,16 @@
     half_green = jnp.einsum(
         "wij,wjm->wim", intersection_inv, orbitals, precision=lax.Precision.HIGHEST
     ).astype(jnp.bfloat16)
-    all_rows = lax.all_gather(factor_rows, "chol", axis=0, tiled=True)
+    ways = lax.axis_size("chol")
+    up = [(d, (d + 1) % ways) for d in range(ways)]
+    down = [(d, (d - 1) % ways) for d in range(ways)]
+    earlier, later = ([factor_rows], [factor_rows])
+    for _ in range(ways // 2):
+        earlier.append(lax.ppermute(earlier[-1], "chol", up))
+    for _ in range((ways - 1) // 2):
+        later.append(lax.ppermute(later[-1], "chol", down))
+    line = jnp.concatenate([*earlier[::-1], *later[1:]], axis=0)
+    all_rows = jnp.roll(line, (lax.axis_index("chol") - ways // 2) * factor_rows.shape[0], axis=0)
     own_density = lax.map(lambda item: density_one(item, all_rows, factor_rotated), half_green)
     density = lax.all_gather(own_density, "chol", axis=0, tiled=True)
     force_bias = lax.dot_general(

time: 249 us -> 302 us (1.21)
  starting transfers between devices: 0.08 us -> 44.7 us
  waiting for transfers between devices: 166 us -> 137 us
  local copies, waits for them, and re-layouts: 2.17 us -> 25.6 us
  blocking collectives: 19.5 us -> 31.5 us
    all_gather x1 -> x0, waiting for transfers between devices: 77.7 us -> none  [on_device(): all_rows = lax.all_gather(factor_rows, 'chol', axis=0, tiled=True)]
    ppermute x0 -> x15, waiting for transfers between devices: none -> 50.1 us  [the longest x8 50 us: on_device(): earlier.append(lax.ppermute(earlier[-1], 'chol', up))]
    ppermute x0 -> x15, starting transfers between devices: none -> 44.6 us  [the longest x8 31.9 us: on_device(): earlier.append(lax.ppermute(earlier[-1], 'chol', up))]
    unnamed x9 -> x68, local copies, waits for them, and re-layouts: 1.2 us -> 24.6 us
    all_gather x1, blocking collectives: 19.5 us -> 31.5 us  [on_device(): density = lax.all_gather(own_density, 'chol', axis=0, tiled=True)]
    dot_general x1, matrix products: 6.26 us -> 2.74 us  [density_one(): lax.dot_general(half_green, all_rows, (((1,), (1,)), ((), ())), preferred...]
  transfers between devices with their start and end apart: 2 -> 16, of which waited for: 2 -> 9; matrix products, arithmetic and copies ran while one was open for 1% -> 5% of each run, Pallas kernels for 0% -> 0%
where the time goes in v1:
time: 302 us; the launch traced here: 300 us
  waiting for transfers between devices  137 us (45%)
  matrix products  46.9 us (16%)
  starting transfers between devices  44.7 us (15%)
  blocking collectives  31.5 us (10%)
  local copies, waits for them, and re-layouts  25.6 us (8%)
  between operations  14.4 us (5%)
    psum x1, waiting for transfers between devices, on_device(): summed_all = lax.psum(partial_sum, 'chol')  87.2 us
    ppermute x8, waiting for transfers between devices, on_device(): earlier.append(lax.ppermute(earlier[-1], 'chol', up))  50 us
    dot_general x4, matrix products, propagate_one(): term = jnp.dot(scaled, all_rows, preferred_element_type=jnp.float32)  40.6 us
    ppermute x8, starting transfers between devices, on_device(): earlier.append(lax.ppermute(earlier[-1], 'chol', up))  31.9 us
    all_gather x1, blocking collectives, on_device(): density = lax.all_gather(own_density, 'chol', axis=0, tiled=True)  31.5 us
    unnamed x68, local copies, waits for them, and re-layouts  24.6 us
    ppermute x7, starting transfers between devices, on_device(): later.append(lax.ppermute(later[-1], 'chol', down))  12.7 us
  transfers between devices with their start and end apart: 16, of which 9 were waited for; matrix products, arithmetic and copies ran while one was open for 5% of the time, Pallas kernels for 0%

profile of v1, /device:TPU:0, one launch (start us, length us, event | category | flops | bytes accessed | tf_op | source)
XLA Modules:
  0.0 300.4 jit_solution(13919923498295640483)
XLA Ops:
  7.2 0.5 collective-permute-start
  7.8 12.1 %collective-permute-done = bf16[256,1024]{1,0:T(8,128)(2,1)S(1)} collective-permute-done((bf16[256,1024]{1,0:T(8,128)(2,1)}, bf16[256,1024]{1,0:T(8,128)(2,1)S(1)}, u32[]{:S(2)}, u32[]{:S(2)}) %collective-permute-start) | collective-permute-done | bytes 524320 | tf_op jit(solution)/shard_map/ppermute | solution.py:42
  19.8 4.4 %collective-permute-start.8 = (bf16[256,1024]{1,0:T(8,128)(2,1)}, bf16[256,1024]{1,0:T(8,128)(2,1)S(1)}, u32[]{:S(2)}, u32[]{:S(2)}) collective-permute-start(bf16[256,1024]{1,0:T(8,128)(2,1)} %param.8), channel_id=1, source_target_pairs={{0,15},{1,0},{2,1},{3,2},{4,3},{5,4},{6,5},{7,6},{8,7},{9,8},{10,9... | collective-permute-start | bytes 1572872 | tf_op jit(solution)/shard_map/ppermute | solution.py:44
  24.3 7.0 %collective-permute-done.1 = bf16[256,1024]{1,0:T(8,128)(2,1)S(1)} collective-permute-done((bf16[256,1024]{1,0:T(8,128)(2,1)S(1)}, bf16[256,1024]{1,0:T(8,128)(2,1)S(1)}, u32[]{:S(2)}, u32[]{:S(2)}) %collective-permute-start.1) | collective-permute-done | bytes 524320 | tf_op jit(solution)/shard_map/ppermute | solution.py:42
  31.3 4.6 %collective-permute-start.9 = (bf16[256,1024]{1,0:T(8,128)(2,1)S(1)}, bf16[256,1024]{1,0:T(8,128)(2,1)S(1)}, u32[]{:S(2)}, u32[]{:S(2)}) collective-permute-start(bf16[256,1024]{1,0:T(8,128)(2,1)S(1)} %collective-permute-done.8), channel_id=1, source_target_pairs={{0,15},{1,0},{2,1},{3,2},{4,3},{5,4},{6,5},{7,6},{8,7},{9,8},{10,9... | collective-permute-start | bytes 1572872 | tf_op jit(solution)/shard_map/ppermute | solution.py:44
  35.9 6.8 %collective-permute-done.2 = bf16[256,1024]{1,0:T(8,128)(2,1)S(1)} collective-permute-done((bf16[256,1024]{1,0:T(8,128)(2,1)S(1)}, bf16[256,1024]{1,0:T(8,128)(2,1)S(1)}, u32[]{:S(2)}, u32[]{:S(2)}) %collective-permute-start.2) | collective-permute-done | bytes 524320 | tf_op jit(solution)/shard_map/ppermute | solution.py:42
  42.7 1.8 collective-permute-start.3
  44.4 2.9 collective-permute-start.10
  47.3 6.8 %collective-permute-done.3 = bf16[256,1024]{1,0:T(8,128)(2,1)S(1)} collective-permute-done((bf16[256,1024]{1,0:T(8,128)(2,1)S(1)}, bf16[256,1024]{1,0:T(8,128)(2,1)S(1)}, u32[]{:S(2)}, u32[]{:S(2)}) %collective-permute-start.3) | collective-permute-done | bytes 524320 | tf_op jit(solution)/shard_map/ppermute | solution.py:42
  54.1 3.8 %collective-permute-start.4 = (bf16[256,1024]{1,0:T(8,128)(2,1)S(1)}, bf16[256,1024]{1,0:T(8,128)(2,1)S(1)}, u32[]{:S(2)}, u32[]{:S(2)}) collective-permute-start(bf16[256,1024]{1,0:T(8,128)(2,1)S(1)} %collective-permute-done.3), channel_id=1, source_target_pairs={{0,1},{1,2},{2,3},{3,4},{4,5},{5,6},{6,7},{7,8},{8,9},{9,10},{10,1... | collective-permute-start | bytes 1572872 | tf_op jit(solution)/shard_map/ppermute | solution.py:42
  57.9 0.7 collective-permute-start.11
  58.6 0.1 copy-done.6
  58.7 6.8 %collective-permute-done.4 = bf16[256,1024]{1,0:T(8,128)(2,1)S(1)} collective-permute-done((bf16[256,1024]{1,0:T(8,128)(2,1)S(1)}, bf16[256,1024]{1,0:T(8,128)(2,1)S(1)}, u32[]{:S(2)}, u32[]{:S(2)}) %collective-permute-start.4) | collective-permute-done | bytes 524320 | tf_op jit(solution)/shard_map/ppermute | solution.py:42
  65.5 6.6 %collective-permute-start.5 = (bf16[256,1024]{1,0:T(8,128)(2,1)S(1)}, bf16[256,1024]{1,0:T(8,128)(2,1)S(1)}, u32[]{:S(2)}, u32[]{:S(2)}) collective-permute-start(bf16[256,1024]{1,0:T(8,128)(2,1)S(1)} %collective-permute-done.4), channel_id=1, source_target_pairs={{0,1},{1,2},{2,3},{3,4},{4,5},{5,6},{6,7},{7,8},{8,9},{9,10},{10,1... | collective-permute-start | bytes 1572872 | tf_op jit(solution)/shard_map/ppermute | solution.py:42
  72.1 0.8 copy-done.8
  72.9 3.9 %collective-permute-done.5 = bf16[256,1024]{1,0:T(8,128)(2,1)S(1)} collective-permute-done((bf16[256,1024]{1,0:T(8,128)(2,1)S(1)}, bf16[256,1024]{1,0:T(8,128)(2,1)S(1)}, u32[]{:S(2)}, u32[]{:S(2)}) %collective-permute-start.5) | collective-permute-done | bytes 524320 | tf_op jit(solution)/shard_map/ppermute | solution.py:42
  76.8 9.6 %collective-permute-start.6 = (bf16[256,1024]{1,0:T(8,128)(2,1)S(1)}, bf16[256,1024]{1,0:T(8,128)(2,1)}, u32[]{:S(2)}, u32[]{:S(2)}) collective-permute-start(bf16[256,1024]{1,0:T(8,128)(2,1)S(1)} %collective-permute-done.5), channel_id=1, source_target_pairs={{0,1},{1,2},{2,3},{3,4},{4,5},{5,6},{6,7},{7,8},{8,9},{9,10},{10,1... | collective-permute-start | bytes 1572872 | tf_op jit(solution)/shard_map/ppermute | solution.py:42
  86.4 4.6 %collective-permute-done.6 = bf16[256,1024]{1,0:T(8,128)(2,1)} collective-permute-done((bf16[256,1024]{1,0:T(8,128)(2,1)S(1)}, bf16[256,1024]{1,0:T(8,128)(2,1)}, u32[]{:S(2)}, u32[]{:S(2)}) %collective-permute-start.6) | collective-permute-done | bytes 524320 | tf_op jit(solution)/shard_map/ppermute | solution.py:42
  91.0 9.6 %collective-permute-start.7 = (bf16[256,1024]{1,0:T(8,128)(2,1)}, bf16[256,1024]{1,0:T(8,128)(2,1)}, u32[]{:S(2)}, u32[]{:S(2)}) collective-permute-start(bf16[256,1024]{1,0:T(8,128)(2,1)} %collective-permute-done.6), channel_id=1, source_target_pairs={{0,1},{1,2},{2,3},{3,4},{4,5},{5,6},{6,7},{7,8},{8,9},{9,10},{10,1... | collective-permute-start | bytes 1572872 | tf_op jit(solution)/shard_map/ppermute | solution.py:42
  100.6 1.7 convolution_convert_fusion
  102.4 2.3 collective-permute-done.7
  104.7 1.1 constant_dynamic-update-slice_fusion.31
  105.7 1.1 constant_dynamic-update-slice_fusion.30
  106.8 1.1 constant_dynamic-update-slice_fusion.29
  107.9 1.1 constant_dynamic-update-slice_fusion.28
  109.0 1.1 constant_dynamic-update-slice_fusion.27
  110.1 1.1 constant_dynamic-update-slice_fusion.26
  111.2 1.1 constant_dynamic-update-slice_fusion.23
  112.4 1.1 constant_dynamic-update-slice_fusion.20
  113.5 1.1 constant_dynamic-update-slice_fusion.19
  114.6 1.1 constant_dynamic-update-slice_fusion.18
  115.7 1.1 constant_dynamic-update-slice_fusion.17
  116.8 1.1 constant_dynamic-update-slice_fusion.15
  117.9 1.1 constant_dynamic-update-slice_fusion.14
  119.6 1.1 constant_dynamic-update-slice_fusion.2
  120.6 1.1 constant_dynamic-update-slice_fusion.1
  121.8 5.7 %copy-done.1 = bf16[8192,1024]{1,0:T(8,128)(2,1)} copy-done((bf16[8192,1024]{1,0:T(8,128)(2,1)}, bf16[8192,1024]{1,0:T(8,128)(2,1)S(1)}, u32[]{:S(2)}) %copy-start.1) | copy-done | bytes 16777240
  127.5 2.7 fusion.7
  130.2 31.5 %all-gather = bf16[65536]{0:T(1024)(128)(2,1)S(1)} all-gather(bf16[4096]{0:T(1024)(128)(2,1)S(1)} %fusion.7), channel_id=2, replica_groups=mesh['parts'=2,'chol'=16] {'chol'}, dimensions={0}, use_global_device_ids=true | all-gather | bytes 139264 | tf_op jit(solution)/shard_map/all_gather | solution.py:48
  161.8 0.3 fusion.60
  162.0 1.6 fusion.47
  163.7 87.2 %all-reduce.2.cloned.1.call-done = f32[16,4096]{1,0:T(8,128)} async-done(((f32[16,4096]{1,0:T(8,128)}), f32[16,4096]{1,0:T(8,128)}) %all-reduce.2.cloned.1.call-update) | async-done | bytes 262160 | tf_op jit(solution)/shard_map/psum | solution.py:54
  250.9 0.9 constant_dynamic-slice_fusion
  251.8 10.7 %fusion.8 = f32[100,1024]{1,0:T(8,128)S(1)} fusion(f32[4096]{0:T(1024)S(1)} %bitcast.25, bf16[8192,1024]{1,0:T(8,128)(2,1)} %copy-done.1, s32[]{:T(128)S(6)} %select_n.17, f32[1,100,1024]{2,0,1:T(1,128)S(1)} %copy-done.2), kind=kOutput, calls=%fused_computation.14 | convolution fusion | flops 1678540800 | bytes 17613824 | tf_op jit(solution)/shard_map/while/body/eval_jaxpr/dot_general | solution.py:27
  262.5 9.9 %fusion.13 = f32[100,1024]{1,0:T(8,128)S(1)} fusion(bf16[8192,1024]{1,0:T(8,128)(2,1)} %copy-done.1, s32[]{:T(128)S(6)} %select_n.17, f32[4096]{0:T(1024)S(1)} %bitcast.26, f32[100,1024]{1,0:T(8,128)S(1)} %fusion.8), kind=kOutput, calls=%fused_computation.19 | convolution fusion | flops 1679052800 | bytes 17613824 | tf_op jit(solution)/shard_map/while/body/eval_jaxpr/dot_general | solution.py:27
  272.4 9.9 %fusion.10 = f32[100,1024]{1,0:T(8,128)S(1)} fusion(bf16[8192,1024]{1,0:T(8,128)(2,1)} %copy-done.1, s32[]{:T(128)S(6)} %select_n.17, f32[4096]{0:T(1024)S(1)} %bitcast.27, f32[100,1024]{1,0:T(8,128)S(1)} %fusion.13), kind=kOutput, calls=%fused_computation.16 | convolution fusion | flops 1679052800 | bytes 17613824 | tf_op jit(solution)/shard_map/while/body/eval_jaxpr/dot_general | solution.py:27
  282.3 10.1 %fusion.31 = f32[1,100,1024]{2,1,0:T(8,128)S(1)} fusion(f32[100,1024]{1,0:T(8,128)S(1)} %fusion.10, f32[100,1024]{1,0:T(8,128)S(1)} %fusion.13, f32[100,1024]{1,0:T(8,128)S(1)} %fusion.8, f32[1,100,1024]{2,0,1:T(1,128)S(1)} %copy-done.2, bf16[8192,1024]{1,0:T(8,128)(2,1)} %copy-done.1, s32[]{:T(128)S(6)} %select_n.17, f32[4096]{0:T(1024)S(1)} %bitcast.28), kind=kOutput, calls=%fused_computation.32 | convolution fusion | flops 1679462400 | bytes 19317760 | tf_op jit(solution)/shard_map/while/body/eval_jaxpr/dot_general | solution.py:27
  292.4 1.2 copy.9
  (65 shorter events, 0.9 us)
Async XLA Ops:
  7.2 154.6 %copy-start = (bf16[64,4096]{1,0:T(8,128)(2,1)S(1)}, bf16[64,4096]{1,0:T(8,128)(2,1)}, u32[]{:S(2)}) copy-start(bf16[64,4096]{1,0:T(8,128)(2,1)} %param.10) | copy-start | bytes 1572868
  7.2 112.1 %copy-start.3 = (bf16[256,1024]{1,0:T(8,128)(2,1)S(1)}, bf16[256,1024]{1,0:T(8,128)(2,1)}, u32[]{:S(2)}) copy-start(bf16[256,1024]{1,0:T(8,128)(2,1)} %param.8) | copy-start | bytes 1572868
  7.2 243.7 %all-reduce.2.cloned.1.call-start = ((), (), s32[]{:S(2)}) async-start(), calls=%async_computation | async-start | bytes 524288 | tf_op jit(solution)/shard_map/psum | solution.py:54
  7.2 12.6 %collective-permute-start = (bf16[256,1024]{1,0:T(8,128)(2,1)}, bf16[256,1024]{1,0:T(8,128)(2,1)S(1)}, u32[]{:S(2)}, u32[]{:S(2)}) collective-permute-start(bf16[256,1024]{1,0:T(8,128)(2,1)} %param.8), channel_id=1, source_target_pairs={{0,1},{1,2},{2,3},{3,4},{4,5},{5,6},{6,7},{7,8},{8,9},{9,10},{10,1... | collective-permute-start | bytes 1572872 | tf_op jit(solution)/shard_map/ppermute | solution.py:42
  19.8 11.4 %collective-permute-start.1 = (bf16[256,1024]{1,0:T(8,128)(2,1)S(1)}, bf16[256,1024]{1,0:T(8,128)(2,1)S(1)}, u32[]{:S(2)}, u32[]{:S(2)}) collective-permute-start(bf16[256,1024]{1,0:T(8,128)(2,1)S(1)} %collective-permute-done), channel_id=1, source_target_pairs={{0,1},{1,2},{2,3},{3,4},{4,5},{5,6},{6,7},{7,8},{8,9},{9,10},{10,1... | collective-permute-start | bytes 1572872 | tf_op jit(solution)/shard_map/ppermute | solution.py:42
  19.8 11.5 %collective-permute-start.8 = (bf16[256,1024]{1,0:T(8,128)(2,1)}, bf16[256,1024]{1,0:T(8,128)(2,1)S(1)}, u32[]{:S(2)}, u32[]{:S(2)}) collective-permute-start(bf16[256,1024]{1,0:T(8,128)(2,1)} %param.8), channel_id=1, source_target_pairs={{0,15},{1,0},{2,1},{3,2},{4,3},{5,4},{6,5},{7,6},{8,7},{9,8},{10,9... | collective-permute-start | bytes 1572872 | tf_op jit(solution)/shard_map/ppermute | solution.py:44
  31.2 11.4 %collective-permute-start.2 = (bf16[256,1024]{1,0:T(8,128)(2,1)S(1)}, bf16[256,1024]{1,0:T(8,128)(2,1)S(1)}, u32[]{:S(2)}, u32[]{:S(2)}) collective-permute-start(bf16[256,1024]{1,0:T(8,128)(2,1)S(1)} %collective-permute-done.1), channel_id=1, source_target_pairs={{0,1},{1,2},{2,3},{3,4},{4,5},{5,6},{6,7},{7,8},{8,9},{9,10},{10,1... | collective-permute-start | bytes 1572872 | tf_op jit(solution)/shard_map/ppermute | solution.py:42
  31.3 13.1 %collective-permute-start.9 = (bf16[256,1024]{1,0:T(8,128)(2,1)S(1)}, bf16[256,1024]{1,0:T(8,128)(2,1)S(1)}, u32[]{:S(2)}, u32[]{:S(2)}) collective-permute-start(bf16[256,1024]{1,0:T(8,128)(2,1)S(1)} %collective-permute-done.8), channel_id=1, source_target_pairs={{0,15},{1,0},{2,1},{3,2},{4,3},{5,4},{6,5},{7,6},{8,7},{9,8},{10,9... | collective-permute-start | bytes 1572872 | tf_op jit(solution)/shard_map/ppermute | solution.py:44
  42.7 15.2 %copy-start.4 = (bf16[256,1024]{1,0:T(8,128)(2,1)}, bf16[256,1024]{1,0:T(8,128)(2,1)S(1)}, u32[]{:S(2)}) copy-start(bf16[256,1024]{1,0:T(8,128)(2,1)S(1)} %collective-permute-done.2) | copy-start | bytes 1572868
  42.7 11.4 %collective-permute-start.3 = (bf16[256,1024]{1,0:T(8,128)(2,1)S(1)}, bf16[256,1024]{1,0:T(8,128)(2,1)S(1)}, u32[]{:S(2)}, u32[]{:S(2)}) collective-permute-start(bf16[256,1024]{1,0:T(8,128)(2,1)S(1)} %collective-permute-done.2), channel_id=1, source_target_pairs={{0,1},{1,2},{2,3},{3,4},{4,5},{5,6},{6,7},{7,8},{8,9},{9,10},{10,1... | collective-permute-start | bytes 1572872 | tf_op jit(solution)/shard_map/ppermute | solution.py:42
  44.4 13.5 %collective-permute-start.10 = (bf16[256,1024]{1,0:T(8,128)(2,1)S(1)}, bf16[256,1024]{1,0:T(8,128)(2,1)S(1)}, u32[]{:S(2)}, u32[]{:S(2)}) collective-permute-start(bf16[256,1024]{1,0:T(8,128)(2,1)S(1)} %collective-permute-done.9), channel_id=1, source_target_pairs={{0,15},{1,0},{2,1},{3,2},{4,3},{5,4},{6,5},{7,6},{8,7},{9,8},{10,9... | collective-permute-start | bytes 1572872 | tf_op jit(solution)/shard_map/ppermute | solution.py:44
  54.1 32.3 %copy-start.10 = (bf16[256,1024]{1,0:T(8,128)(2,1)}, bf16[256,1024]{1,0:T(8,128)(2,1)S(1)}, u32[]{:S(2)}) copy-start(bf16[256,1024]{1,0:T(8,128)(2,1)S(1)} %collective-permute-done.3) | copy-start | bytes 1572868
  54.1 11.4 %collective-permute-start.4 = (bf16[256,1024]{1,0:T(8,128)(2,1)S(1)}, bf16[256,1024]{1,0:T(8,128)(2,1)S(1)}, u32[]{:S(2)}, u32[]{:S(2)}) collective-permute-start(bf16[256,1024]{1,0:T(8,128)(2,1)S(1)} %collective-permute-done.3), channel_id=1, source_target_pairs={{0,1},{1,2},{2,3},{3,4},{4,5},{5,6},{6,7},{7,8},{8,9},{9,10},{10,1... | collective-permute-start | bytes 1572872 | tf_op jit(solution)/shard_map/ppermute | solution.py:42
  57.9 0.8 copy-start.6
  57.9 14.2 %collective-permute-start.11 = (bf16[256,1024]{1,0:T(8,128)(2,1)S(1)}, bf16[256,1024]{1,0:T(8,128)(2,1)S(1)}, u32[]{:S(2)}, u32[]{:S(2)}) collective-permute-start(bf16[256,1024]{1,0:T(8,128)(2,1)S(1)} %collective-permute-done.10), channel_id=1, source_target_pairs={{0,15},{1,0},{2,1},{3,2},{4,3},{5,4},{6,5},{7,6},{8,7},{9,8},{10,9... | collective-permute-start | bytes 1572872 | tf_op jit(solution)/shard_map/ppermute | solution.py:44
  65.5 20.9 %copy-start.12 = (bf16[256,1024]{1,0:T(8,128)(2,1)}, bf16[256,1024]{1,0:T(8,128)(2,1)S(1)}, u32[]{:S(2)}) copy-start(bf16[256,1024]{1,0:T(8,128)(2,1)S(1)} %collective-permute-done.4) | copy-start | bytes 1572868
  65.5 11.3 %collective-permute-start.5 = (bf16[256,1024]{1,0:T(8,128)(2,1)S(1)}, bf16[256,1024]{1,0:T(8,128)(2,1)S(1)}, u32[]{:S(2)}, u32[]{:S(2)}) collective-permute-start(bf16[256,1024]{1,0:T(8,128)(2,1)S(1)} %collective-permute-done.4), channel_id=1, source_target_pairs={{0,1},{1,2},{2,3},{3,4},{4,5},{5,6},{6,7},{7,8},{8,9},{9,10},{10,1... | collective-permute-start | bytes 1572872 | tf_op jit(solution)/shard_map/ppermute | solution.py:42
  72.1 0.8 copy-start.8
  72.9 13.4 %collective-permute-start.12 = (bf16[256,1024]{1,0:T(8,128)(2,1)S(1)}, bf16[256,1024]{1,0:T(8,128)(2,1)}, u32[]{:S(2)}, u32[]{:S(2)}) collective-permute-start(bf16[256,1024]{1,0:T(8,128)(2,1)S(1)} %collective-permute-done.11), channel_id=1, source_target_pairs={{0,15},{1,0},{2,1},{3,2},{4,3},{5,4},{6,5},{7,6},{8,7},{9,8},{10,9... | collective-permute-start | bytes 1572872 | tf_op jit(solution)/shard_map/ppermute | solution.py:44
  76.8 14.2 %copy-start.14 = (bf16[256,1024]{1,0:T(8,128)(2,1)}, bf16[256,1024]{1,0:T(8,128)(2,1)S(1)}, u32[]{:S(2)}) copy-start(bf16[256,1024]{1,0:T(8,128)(2,1)S(1)} %collective-permute-done.5) | copy-start | bytes 1572868
  76.8 14.2 %collective-permute-start.6 = (bf16[256,1024]{1,0:T(8,128)(2,1)S(1)}, bf16[256,1024]{1,0:T(8,128)(2,1)}, u32[]{:S(2)}, u32[]{:S(2)}) collective-permute-start(bf16[256,1024]{1,0:T(8,128)(2,1)S(1)} %collective-permute-done.5), channel_id=1, source_target_pairs={{0,1},{1,2},{2,3},{3,4},{4,5},{5,6},{6,7},{7,8},{8,9},{9,10},{10,1... | collective-permute-start | bytes 1572872 | tf_op jit(solution)/shard_map/ppermute | solution.py:42
  86.3 16.0 %collective-permute-start.13 = (bf16[256,1024]{1,0:T(8,128)(2,1)}, bf16[256,1024]{1,0:T(8,128)(2,1)}, u32[]{:S(2)}, u32[]{:S(2)}) collective-permute-start(bf16[256,1024]{1,0:T(8,128)(2,1)} %collective-permute-done.12), channel_id=1, source_target_pairs={{0,15},{1,0},{2,1},{3,2},{4,3},{5,4},{6,5},{7,6},{8,7},{9,8},{10,9... | collective-permute-start | bytes 1572872 | tf_op jit(solution)/shard_map/ppermute | solution.py:44
  91.0 13.7 %collective-permute-start.7 = (bf16[256,1024]{1,0:T(8,128)(2,1)}, bf16[256,1024]{1,0:T(8,128)(2,1)}, u32[]{:S(2)}, u32[]{:S(2)}) collective-permute-start(bf16[256,1024]{1,0:T(8,128)(2,1)} %collective-permute-done.6), channel_id=1, source_target_pairs={{0,1},{1,2},{2,3},{3,4},{4,5},{5,6},{6,7},{7,8},{8,9},{9,10},{10,1... | collective-permute-start | bytes 1572872 | tf_op jit(solution)/shard_map/ppermute | solution.py:42
  100.6 18.5 %copy-start.15 = (bf16[256,1024]{1,0:T(8,128)(2,1)S(1)}, bf16[256,1024]{1,0:T(8,128)(2,1)}, u32[]{:S(2)}) copy-start(bf16[256,1024]{1,0:T(8,128)(2,1)} %copy-done.14) | copy-start | bytes 1572868
  100.6 18.5 %copy-start.13 = (bf16[256,1024]{1,0:T(8,128)(2,1)S(1)}, bf16[256,1024]{1,0:T(8,128)(2,1)}, u32[]{:S(2)}) copy-start(bf16[256,1024]{1,0:T(8,128)(2,1)} %copy-done.12) | copy-start | bytes 1572868
  100.6 18.6 %copy-start.11 = (bf16[256,1024]{1,0:T(8,128)(2,1)S(1)}, bf16[256,1024]{1,0:T(8,128)(2,1)}, u32[]{:S(2)}) copy-start(bf16[256,1024]{1,0:T(8,128)(2,1)} %copy-done.10) | copy-start | bytes 1572868
  100.6 18.6 %copy-start.5 = (bf16[256,1024]{1,0:T(8,128)(2,1)S(1)}, bf16[256,1024]{1,0:T(8,128)(2,1)}, u32[]{:S(2)}) copy-start(bf16[256,1024]{1,0:T(8,128)(2,1)} %copy-done.4) | copy-start | bytes 1572868
  100.6 18.9 %copy-start.7 = (bf16[256,1024]{1,0:T(8,128)(2,1)S(1)}, bf16[256,1024]{1,0:T(8,128)(2,1)}, u32[]{:S(2)}) copy-start(bf16[256,1024]{1,0:T(8,128)(2,1)} %copy-done.6) | copy-start | bytes 1572868
  100.6 18.9 %copy-start.9 = (bf16[256,1024]{1,0:T(8,128)(2,1)S(1)}, bf16[256,1024]{1,0:T(8,128)(2,1)}, u32[]{:S(2)}) copy-start(bf16[256,1024]{1,0:T(8,128)(2,1)} %copy-done.8) | copy-start | bytes 1572868
  102.3 25.2 %copy-start.17 = (bf16[100,4096]{1,0:T(8,128)(2,1)S(1)}, bf16[100,4096]{1,0:T(8,128)(2,1)}, u32[]{:S(2)}) copy-start(bf16[100,4096]{1,0:T(8,128)(2,1)} %param.9) | copy-start | bytes 2457604
  102.3 14.5 %collective-permute-start.14 = (bf16[256,1024]{1,0:T(8,128)(2,1)}, bf16[256,1024]{1,0:T(8,128)(2,1)S(1)}, u32[]{:S(2)}, u32[]{:S(2)}) collective-permute-start(bf16[256,1024]{1,0:T(8,128)(2,1)} %collective-permute-done.13), channel_id=1, source_target_pairs={{0,15},{1,0},{2,1},{3,2},{4,3},{5,4},{6,5},{7,6},{8,7},{9,8},{10,9... | collective-permute-start | bytes 1572872 | tf_op jit(solution)/shard_map/ppermute | solution.py:44
  115.6 136.1 %copy-start.2 = (f32[1,100,1024]{2,0,1:T(1,128)S(1)}, f32[1,100,1024]{2,0,1:T(1,128)}, u32[]{:S(2)}) copy-start(f32[1,100,1024]{2,0,1:T(1,128)} %param.6) | copy-start | bytes 1228804
  121.8 5.7 %copy-start.1 = (bf16[8192,1024]{1,0:T(8,128)(2,1)}, bf16[8192,1024]{1,0:T(8,128)(2,1)S(1)}, u32[]{:S(2)}) copy-start(bf16[8192,1024]{1,0:T(8,128)(2,1)S(1)} %constant_dynamic-update-slice_fusion) | copy-start | bytes 50331652
  162.0 110.3 %copy-start.16 = (f32[16,64]{1,0:T(8,128)}, f32[16,64]{1,0:T(8,128)S(1)}, u32[]{:S(2)}) copy-start(f32[16,64]{1,0:T(8,128)S(1)} %fusion.60) | copy-start | bytes 12292
Sparse Core Ops, SparseCore 0:
  163.8 87.0 all-reduce.1
